TPU v7x, 32 devices: a whole 2x2x4 slice. The times are simulated.
32 devices in a mesh: dp: 2 (over core), ctx: 4 (over y, x), hd: 4 (over z).
Axes of the slice: x: 2, y: 2, z: 4, core: 2. Of those that a mesh axis runs over, the one named last changes fastest.
Arguments:
- tokens_in: bfloat16 [4, 2048, 1536], P('dp', ('ctx', 'hd')), may hold values from -6 to 6
- seg_ids: int32 [4, 2048], P('dp'), may hold values from 0 to 7, never falling along the last dimension, each value on 1 to 512 neighbouring positions
- in_norm: float32 [1536], replicated, may hold values from 0.5 to 1.5
- z_proj: bfloat16 [1536, 3072], P(('dp', 'ctx', 'hd')), may hold values from -0.15625 to 0.15625
- xbc_proj: bfloat16 [1536, 3328], P(('dp', 'ctx', 'hd')), may hold values from -0.15625 to 0.15625
- dt_proj: bfloat16 [1536, 48], P(('dp', 'ctx', 'hd')), may hold values from -0.0390625 to 0.0390625
- conv_taps: float32 [4, 3328], replicated, may hold values from -3 to 3
- conv_bias: float32 [3328], replicated, may hold values from -2 to 2
- dt_bias: float32 [48], replicated, may hold values from -9 to -2
- a_log: float32 [48], replicated, may hold values from 0 to 2.77
- d_skip: float32 [48], replicated, may hold values from 0.5 to 2
- gate_norm: float32 [3072], replicated, may hold values from 0.5 to 1.5
- out_proj: bfloat16 [3072, 1536], P(('dp', 'ctx', 'hd')), may hold values from -0.109375 to 0.109375
- out_cotangent: bfloat16 [4, 2048, 1536], P('dp', ('ctx', 'hd')), may hold values from -6 to 6
Outputs:
- layer_out: bfloat16 [4, 2048, 1536], P('dp', ('ctx', 'hd'))
- tokens_grad: float32 [4, 2048, 1536], P('dp', ('ctx', 'hd'))
- in_norm_grad: float32 [1536], replicated
- z_proj_grad: float32 [1536, 3072], P(('dp', 'ctx', 'hd'))
- xbc_proj_grad: float32 [1536, 3328], P(('dp', 'ctx', 'hd'))
- dt_proj_grad: float32 [1536, 48], P(('dp', 'ctx', 'hd'))
- conv_taps_grad: float32 [4, 3328], replicated
- conv_bias_grad: float32 [3328], replicated
- dt_bias_grad: float32 [48], replicated
- a_log_grad: float32 [48], replicated
- d_skip_grad: float32 [48], replicated
- gate_norm_grad: float32 [3072], replicated
- out_proj_grad: float32 [3072, 1536], P(('dp', 'ctx', 'hd'))
Inputs may be any that keep to these rules, and one draw needn't show every extreme that they name: `seg_ids`: along each sequence the document numbers never fall; each document has 1 to 512 tokens and one has exactly that many.
All inputs are finite; a program needn't handle non-finite values.
Results may differ from a plain program's by a relative error of at most 0.0097.
Values may be sent and summed in bfloat16 or wider, within the bound.
No kernel may reach another device: no remote copies, remote signals or barrier semaphores. Data moves between devices by JAX's collectives and lax.ppermute only.
A program may use at most 320 MiB of HBM per device.

v0:
```python
import jax
import jax.numpy as jnp
from jax import lax
from jax.sharding import PartitionSpec as P

H = 48
P_SIZE = 64
N = 128
KW = 4
Q = 256
DI = 3072
HIGH = lax.Precision.HIGHEST
EPS = 1e-05


def from_behind(shard, axis, by):
    count = lax.axis_size(axis)
    pairs = [(i, i + by) for i in range(count) if 0 <= i + by < count]
    return lax.ppermute(shard, axis, pairs)


def carried_in(shard, axis, combine, identity, reverse):
    count, place = (lax.axis_size(axis), lax.axis_index(axis))
    everything = jax.tree.map(
        lambda part, kind: lax.all_gather(part.astype(kind), axis),
        shard,
        (jnp.bfloat16, jnp.bfloat16),
    )
    start = jax.tree.map(
        lambda part, zero: jnp.broadcast_to(jnp.asarray(zero, part.dtype), part.shape),
        shard,
        identity,
    )

    def turn(k, before):
        at = count - 1 - k if reverse else k
        reached = at > place if reverse else at < place
        new = combine(
            before, jax.tree.map(lambda part, own: part[at].astype(own.dtype), everything, shard)
        )
        return jax.tree.map(lambda a, b: jnp.where(reached, a, b), new, before)

    return lax.fori_loop(0, count, turn, start)


def norm_rows(values, gain):
    return values * lax.rsqrt(jnp.mean(values * values, axis=-1, keepdims=True) + EPS) * gain


def gate_tail(mixer_val, gate_val, gain):
    return norm_rows(mixer_val * jax.nn.silu(gate_val), gain)


def conv_act(padded, taps, bias, masks):
    length = masks.shape[1]
    mixed = bias
    for tap in range(taps.shape[0]):
        mixed = mixed + taps[tap] * padded[tap : tap + length] * masks[tap][:, None]
    return jax.nn.silu(mixed)


def back_dot(grad_val, weight):
    return lax.dot_general(
        grad_val, weight, (((1,), (1,)), ((), ())), preferred_element_type=jnp.float32
    )


def compose(earlier, later):
    return (earlier[0] * later[0], later[0][:, None, None] * earlier[1] + later[1])


def block_decay(rate_val, bias_here, decay_log, seg_blk, seg_before):
    log_rate = jax.nn.softplus(rate_val + bias_here) * -jnp.exp(decay_log)
    cumul = jnp.cumsum(log_rate, axis=0)
    keep = (seg_blk == seg_before).astype(jnp.float32)
    lead = jnp.exp(cumul) * keep[:, None]
    return (lead[-1], lead)


def block_ssd(
    x_val,
    rate_val,
    bias_here,
    decay_log,
    skip_here,
    bc_val,
    state_in,
    seg_blk,
    seg_before,
    span_len,
):
    length, heads = rate_val.shape
    count = length // span_len
    width_n = bc_val.shape[1] // 2
    x_groups = x_val.reshape(count, span_len, heads, -1)
    dt_groups = jax.nn.softplus(rate_val + bias_here).reshape(count, span_len, heads)
    cumul = jnp.cumsum(dt_groups * -jnp.exp(decay_log), axis=1)
    b_groups = bc_val[:, :width_n].reshape(count, span_len, width_n)
    c_groups = bc_val[:, width_n:].reshape(count, span_len, width_n)
    seg_groups = seg_blk.reshape(count, span_len)
    before = jnp.concatenate([seg_before, seg_groups[:-1, -1]])
    order = jnp.arange(span_len)
    mask = (seg_groups[:, :, None] == seg_groups[:, None, :]) & (order[:, None] >= order[None, :])
    gaps = cumul[:, :, None, :] - cumul[:, None, :, :]
    decay = jnp.exp(jnp.where(mask[..., None], gaps, 0.0)) * mask[..., None].astype(jnp.float32)
    scores = jnp.einsum("ctn,csn->cts", c_groups, b_groups, precision=HIGH)
    mix_w = scores[..., None] * decay * dt_groups[:, None, :, :]
    y_part = jnp.einsum("ctsh,cshp->cthp", mix_w, x_groups, precision=HIGH)
    keep = (seg_groups == before[:, None]).astype(jnp.float32)
    lead = jnp.exp(cumul) * keep[..., None]
    tail = (
        jnp.exp(cumul[:, -1:, :] - cumul)
        * (seg_groups == seg_groups[:, -1:]).astype(jnp.float32)[..., None]
        * dt_groups
    )
    pieces = jnp.einsum("csh,cshp,csn->chpn", tail, x_groups, b_groups, precision=HIGH)

    def advance(state, item):
        piece, factor = item
        return (state * factor[:, None, None] + piece, state)

    state_end, entering = lax.scan(advance, state_in, (pieces, lead[:, -1, :]))
    y_part = y_part + lead[..., None] * jnp.einsum(
        "ctn,chpn->cthp", c_groups, entering, precision=HIGH
    )
    y_part = y_part + skip_here[:, None] * x_groups
    return (y_part.reshape(length, -1), state_end)


def shards(
    tokens_in,
    seg_ids,
    in_norm,
    z_proj,
    xbc_proj,
    dt_proj,
    conv_taps,
    conv_bias,
    dt_bias,
    a_log,
    d_skip,
    gate_norm,
    out_proj,
    out_cotangent,
):
    batches, rows, width = tokens_in.shape
    n_heads_axis = lax.axis_size("hd")
    heads_here = H // n_heads_axis
    block = rows * n_heads_axis
    channels = DI + 2 * N
    start_tok = lax.axis_index(("ctx", "hd")) * rows
    start_blk = lax.axis_index("ctx") * block
    head_low = lax.axis_index("hd") * heads_here
    bias_here = lax.dynamic_slice_in_dim(dt_bias, head_low, heads_here)
    decay_log = lax.dynamic_slice_in_dim(a_log, head_low, heads_here)
    skip_here = lax.dynamic_slice_in_dim(d_skip, head_low, heads_here)
    unit = (jnp.ones((heads_here,), jnp.float32), jnp.zeros((heads_here, P_SIZE, N), jnp.float32))

    def fetch():
        return (
            lax.all_gather(z_proj, ("dp", "ctx", "hd"), axis=0, tiled=True),
            lax.all_gather(xbc_proj, ("dp", "ctx", "hd"), axis=0, tiled=True),
            lax.all_gather(dt_proj, ("dp", "ctx", "hd"), axis=0, tiled=True),
            lax.all_gather(out_proj, ("dp", "ctx", "hd"), axis=0, tiled=True),
        )

    stored = []
    outputs = []
    for batch in range(batches):
        zed_weight, xbc_weight, rate_weight, out_weight = fetch()
        seg_row = seg_ids[batch]
        seg_pad = jnp.concatenate([jnp.full((KW - 1,), -1, jnp.int32), seg_row])
        seg_near = lax.dynamic_slice_in_dim(seg_pad, start_tok, rows + KW - 1)
        seg_own = seg_near[KW - 1 :]
        masks = jnp.stack([seg_near[tap : tap + rows] == seg_own for tap in range(KW)]).astype(
            jnp.float32
        )
        seg_blk = lax.dynamic_slice_in_dim(seg_row, start_blk, block)
        seg_before = lax.dynamic_slice_in_dim(seg_pad, start_blk + KW - 2, 1)
        source = tokens_in[batch].astype(jnp.float32)
        normed = norm_rows(source, in_norm).astype(jnp.bfloat16)
        gate_in = jnp.dot(normed, zed_weight, preferred_element_type=jnp.float32)
        raw_xbc = jnp.dot(normed, xbc_weight, preferred_element_type=jnp.float32).astype(
            jnp.bfloat16
        )
        rate_raw = jnp.dot(normed, rate_weight, preferred_element_type=jnp.float32).astype(
            jnp.bfloat16
        )
        rim_rows = from_behind(raw_xbc[rows - (KW - 1) :], ("ctx", "hd"), 1)
        padded = jnp.concatenate([rim_rows, raw_xbc], 0).astype(jnp.float32)
        active = conv_act(padded, conv_taps, conv_bias, masks)
        x_low = active[:, :DI].astype(jnp.bfloat16)
        bc_low = active[:, DI:].astype(jnp.bfloat16)
        x_heads, rate_heads = (
            lax.all_to_all(x_low, "hd", split_axis=1, concat_axis=0, tiled=True),
            lax.all_to_all(rate_raw, "hd", split_axis=1, concat_axis=0, tiled=True),
        )
        bc_all = lax.all_gather(bc_low, "hd", axis=0, tiled=True)
        x_float = x_heads.astype(jnp.float32)
        rate_float = rate_heads.astype(jnp.float32)
        bc_float = bc_all.astype(jnp.float32)
        zero_state = jnp.zeros((heads_here, P_SIZE, N), jnp.float32)
        y_zero, state_local = block_ssd(
            x_float,
            rate_float,
            bias_here,
            decay_log,
            skip_here,
            bc_float,
            zero_state,
            seg_blk,
            seg_before,
            Q,
        )
        total_decay, lead_blk = block_decay(rate_float, bias_here, decay_log, seg_blk, seg_before)
        unused, state_in = carried_in((total_decay, state_local), "ctx", compose, unit, False)
        carried = lead_blk[:, :, None] * jnp.einsum(
            "tn,hpn->thp", bc_float[:, N:], state_in, precision=HIGH
        )
        y_heads = y_zero + carried.reshape(block, -1)
        y_tokens = lax.all_to_all(
            y_heads.astype(jnp.bfloat16), "hd", split_axis=0, concat_axis=1, tiled=True
        )
        y_float = y_tokens.astype(jnp.float32)
        gated = gate_tail(y_float, gate_in, gate_norm).astype(jnp.bfloat16)
        result = source + jnp.dot(gated, out_weight, preferred_element_type=jnp.float32)
        outputs.append(result.astype(jnp.bfloat16))
        stored.append(
            (
                source,
                normed,
                gate_in,
                padded,
                masks,
                x_float,
                rate_float,
                bc_float,
                seg_blk,
                seg_before,
                lead_blk,
                total_decay,
                state_in,
                y_float,
                gated,
            )
        )
    grads_tok = []
    normed_rows = []
    proj_grads = []
    gated_rows = []
    cot_rows = []
    norm_total = jnp.zeros((width,), jnp.float32)
    taps_total = jnp.zeros(conv_taps.shape, jnp.float32)
    cbias_total = jnp.zeros((channels,), jnp.float32)
    dtb_total = jnp.zeros((H,), jnp.float32)
    alog_total = jnp.zeros((H,), jnp.float32)
    skip_total = jnp.zeros((H,), jnp.float32)
    gate_total = jnp.zeros((DI,), jnp.float32)
    for batch in range(batches):
        zed_weight, xbc_weight, rate_weight, out_weight = fetch()
        (
            source,
            normed,
            gate_in,
            padded,
            masks,
            x_float,
            rate_float,
            bc_float,
            seg_blk,
            seg_before,
            lead_blk,
            total_decay,
            state_in,
            y_float,
            gated,
        ) = stored[batch]
        cot_low = out_cotangent[batch]
        d_gated = back_dot(cot_low, out_weight)
        unused, tail_pull = jax.vjp(gate_tail, y_float, gate_in, gate_norm)
        d_mixer, d_gate_in, d_gain = tail_pull(d_gated)
        d_mixer_heads = lax.all_to_all(
            d_mixer.astype(jnp.bfloat16), "hd", split_axis=1, concat_axis=0, tiled=True
        )
        d_y_float = d_mixer_heads.astype(jnp.float32)
        d_local = jnp.einsum(
            "th,thp,tn->hpn",
            lead_blk,
            d_y_float.reshape(block, heads_here, P_SIZE),
            bc_float[:, N:],
            precision=HIGH,
        )
        unused, d_end = carried_in((total_decay, d_local), "ctx", compose, unit, True)

        def with_state(x_value, rate_value, bias_value, decay_value, skip_value, bc_value):
            return block_ssd(
                x_value,
                rate_value,
                bias_value,
                decay_value,
                skip_value,
                bc_value,
                state_in,
                seg_blk,
                seg_before,
                Q,
            )

        unused, ssd_pull = jax.vjp(
            with_state, x_float, rate_float, bias_here, decay_log, skip_here, bc_float
        )
        d_x_heads, d_rate_heads, d_bias_h, d_decay_h, d_skip_h, d_bc_heads = ssd_pull(
            (d_y_float, d_end)
        )
        d_x_tok, d_rate_tok = (
            lax.all_to_all(
                d_x_heads.astype(jnp.bfloat16), "hd", split_axis=0, concat_axis=1, tiled=True
            ),
            lax.all_to_all(
                d_rate_heads.astype(jnp.bfloat16), "hd", split_axis=0, concat_axis=1, tiled=True
            ),
        )
        d_bc_tok = lax.psum_scatter(
            d_bc_heads.astype(jnp.bfloat16), "hd", scatter_dimension=0, tiled=True
        ).astype(jnp.float32)
        d_active = jnp.concatenate([d_x_tok.astype(jnp.float32), d_bc_tok], axis=1)

        def conv_here(pad_value, taps_value, bias_value):
            return conv_act(pad_value, taps_value, bias_value, masks)

        unused, conv_pull = jax.vjp(conv_here, padded, conv_taps, conv_bias)
        d_padded, d_taps, d_cbias = conv_pull(d_active)
        back_rim = from_behind(d_padded[: KW - 1].astype(jnp.bfloat16), ("ctx", "hd"), -1).astype(
            jnp.float32
        )
        d_raw = d_padded[KW - 1 :] + jnp.concatenate(
            [jnp.zeros((rows - (KW - 1), channels), jnp.float32), back_rim], 0
        )
        d_raw_low = d_raw.astype(jnp.bfloat16)
        d_gate_low = d_gate_in.astype(jnp.bfloat16)
        d_normed = (
            back_dot(d_gate_low, zed_weight)
            + back_dot(d_raw_low, xbc_weight)
            + back_dot(d_rate_tok, rate_weight)
        )
        unused, norm_pull = jax.vjp(norm_rows, source, in_norm)
        d_source, d_norm_gain = norm_pull(d_normed)
        grads_tok.append(d_source + cot_low.astype(jnp.float32))
        normed_rows.append(normed)
        proj_grads.append(jnp.concatenate([d_gate_low, d_raw_low, d_rate_tok], axis=1))
        gated_rows.append(gated)
        cot_rows.append(cot_low)
        norm_total = norm_total + d_norm_gain
        taps_total = taps_total + d_taps
        cbias_total = cbias_total + d_cbias
        dtb_total = dtb_total + lax.dynamic_update_slice_in_dim(
            jnp.zeros((H,), jnp.float32), d_bias_h, head_low, 0
        )
        alog_total = alog_total + lax.dynamic_update_slice_in_dim(
            jnp.zeros((H,), jnp.float32), d_decay_h, head_low, 0
        )
        skip_total = skip_total + lax.dynamic_update_slice_in_dim(
            jnp.zeros((H,), jnp.float32), d_skip_h, head_low, 0
        )
        gate_total = gate_total + d_gain
    normed_all = jnp.concatenate(normed_rows, 0)
    proj_all = jnp.concatenate(proj_grads, 0)
    gated_all = jnp.concatenate(gated_rows, 0)
    cot_all = jnp.concatenate(cot_rows, 0)
    part = normed_all
    in_grad = lax.psum_scatter(
        lax.dot_general(
            part, proj_all, (((0,), (0,)), ((), ())), preferred_element_type=jnp.float32
        ),
        ("dp", "ctx", "hd"),
        scatter_dimension=0,
        tiled=True,
    )
    part = gated_all
    out_grad = lax.psum_scatter(
        lax.dot_general(
            part, cot_all, (((0,), (0,)), ((), ())), preferred_element_type=jnp.float32
        ),
        ("dp", "ctx", "hd"),
        scatter_dimension=0,
        tiled=True,
    )
    norm_sum, taps_sum, cbias_sum, dtb_sum, alog_sum, skip_sum, gate_sum = lax.psum(
        (norm_total, taps_total, cbias_total, dtb_total, alog_total, skip_total, gate_total),
        ("dp", "ctx", "hd"),
    )
    return (
        jnp.stack(outputs),
        jnp.stack(grads_tok),
        norm_sum,
        in_grad[:, :DI],
        in_grad[:, DI : DI + channels],
        in_grad[:, DI + channels :],
        taps_sum,
        cbias_sum,
        dtb_sum,
        alog_sum,
        skip_sum,
        gate_sum,
        out_grad,
    )


def solution(mesh):
    in_specs = (
        P("dp", ("ctx", "hd"), None),
        P("dp", None),
        P(),
        P(("dp", "ctx", "hd"), None),
        P(("dp", "ctx", "hd"), None),
        P(("dp", "ctx", "hd"), None),
        P(),
        P(),
        P(),
        P(),
        P(),
        P(),
        P(("dp", "ctx", "hd"), None),
        P("dp", ("ctx", "hd"), None),
    )
    out_specs = (
        P("dp", ("ctx", "hd"), None),
        P("dp", ("ctx", "hd"), None),
        P(),
        P(("dp", "ctx", "hd"), None),
        P(("dp", "ctx", "hd"), None),
        P(("dp", "ctx", "hd"), None),
        P(),
        P(),
        P(),
        P(),
        P(),
        P(),
        P(("dp", "ctx", "hd"), None),
    )
    return jax.shard_map(shards, mesh=mesh, in_specs=in_specs, out_specs=out_specs, check_vma=False)
```

profile of v0, /device:TPU:0, one launch (start us, length us, event | category | flops | bytes accessed | tf_op | source)
XLA Modules:
  0.0 1491.1 jit_solution(12795185626710274791)
XLA Ops:
  8.7 76.8 %all_gather.68 = bf16[1536,48]{1,0:T(8,128)(2,1)S(1)} all-gather(bf16[48,48]{1,0:T(8,128)(2,1)} %param.40), channel_id=1, replica_groups=mesh['dp'=2,'ctx'=4,'hd'=4] {'dp','ctx','hd'}, dimensions={0}, use_global_device_ids=true | all-gather | bytes 152064 | tf_op jit(solution)/shard_map/all_gather | solution.py:163
  125.4 14.0 all-gather.5
  173.7 6.7 all-to-all-start.3
  188.7 17.7 %all_gather.74 = bf16[512,256]{1,0:T(8,128)(2,1)S(1)} all-gather(bf16[128,256]{1,0:T(8,128)(2,1)S(1)} %slice.403), channel_id=1, replica_groups=mesh['dp'=2,'ctx'=4,'hd'=4] {'hd'}, dimensions={0}, use_global_device_ids=true | all-gather | bytes 327680 | tf_op jit(solution)/shard_map/all_gather | solution.py:198
  206.4 15.0 %all_gather.33 = bf16[512,256]{1,0:T(8,128)(2,1)S(1)} all-gather(bf16[128,256]{1,0:T(8,128)(2,1)S(1)} %slice.386), channel_id=1, replica_groups=mesh['dp'=2,'ctx'=4,'hd'=4] {'hd'}, dimensions={0}, use_global_device_ids=true | all-gather | bytes 327680 | tf_op jit(solution)/shard_map/all_gather | solution.py:198
  238.3 7.7 while.156
  247.1 12.9 all-gather.1
  260.0 6.8 while.157
  289.1 14.6 all-to-all-start.5
  313.3 7.6 while.154
  321.9 11.6 all-gather
  336.4 6.8 while.155
  343.1 7.1 fusion.101
  393.6 7.3 multiply_reduce_fusion.19
  401.5 9.2 multiply_reduce_fusion.13
  410.8 7.1 multiply_reduce_fusion.18
  418.0 9.1 multiply_convert_fusion.3
  446.5 13.0 all-to-all-done.9
  472.3 10.0 all-gather.3
  495.6 7.8 while.153
  524.5 12.2 all-gather.2
  553.0 6.8 while.151
  708.2 16.6 %reduce-scatter.5.cloned.1.call-done = bf16[128,256]{1,0:T(8,128)(2,1)} async-done(((bf16[512,256]{1,0:T(8,128)(2,1)}), bf16[128,256]{1,0:T(8,128)(2,1)}) %reduce-scatter.5.cloned.1.call-update) | async-done | bytes 65552 | tf_op jit(solution)/shard_map/reduce_scatter | solution.py:323
  741.9 19.9 %fusion.38 = f32[1536,6448]{1,0:T(8,128)} fusion(bf16[128,48]{1,0:T(8,128)(2,1)S(1)} %copy.500, bf16[128,3328]{1,0:T(8,128)(2,1)S(1)} %fusion.98, bf16[128,3072]{1,0:T(8,128)(2,1)S(1)} %copy-done.28, bf16[128,48]{1,0:T(8,128)(2,1)S(1)} %copy-done.103, bf16[128,3328]{1,0:T(8,128)(2,1)S(1)} %fusion.99, bf16[128,3072]{1,0:T(8,128)(2,1)} %get-tuple-element.1175, ...), kind=kOutput, calls=%fused_computation.78 | convolution fusion | flops 5092294656 | bytes 43704320 | tf_op jit(solution)/shard_map/dot_general | solution.py:372
  764.4 7.0 fusion.278
  771.4 9.5 fusion.276
  788.5 8.9 convolution_add_fusion.2
  798.7 9.0 convolution_add_fusion.3
  809.9 11.9 fusion.118
  836.5 293.6 %reduce-scatter.9.cloned.1.call-done = f32[48,6448]{1,0:T(8,128)} async-done(((f32[1536,6448]{1,0:T(8,128)}), f32[48,6448]{1,0:T(8,128)}) %reduce-scatter.9.cloned.1.call-update) | async-done | bytes 1238032 | tf_op jit(solution)/shard_map/reduce_scatter | solution.py:371
  1135.3 125.0 %all-reduce.31.cloned.1.call-done = (f32[1536]{0:T(1024)}, f32[4,3328]{1,0:T(4,128)}, f32[3328]{0:T(1024)}, f32[48]{0:T(128)}, f32[48]{0:T(128)}, /*index=5*/f32[48]{0:T(128)}, f32[3072]{0:T(1024)}) async-done(((f32[1536]{0:T(1024)}, f32[4,3328]{1,0:T(4,128)}, f32[3328]{0:T(1024)}, f32[48]{0:T(128)}, f32[48]{0:T(128)}, /*index=5*/f32[48]{0:T(128)}, f32[3072]{0:T(1024)}), (f32[1536]{0:T(1024)}, ...) | async-done | bytes 85584 | tf_op jit(solution)/shard_map/psum | solution.py:388
  1260.2 214.8 %reduce-scatter.11.cloned.1.call-done = f32[96,1536]{1,0:T(8,128)} async-done(((f32[3072,1536]{1,0:T(8,128)}), f32[96,1536]{1,0:T(8,128)}) %reduce-scatter.11.cloned.1.call-update) | async-done | bytes 589840 | tf_op jit(solution)/shard_map/reduce_scatter | solution.py:380
  (846 shorter events, 530.4 us)
Async XLA Ops:
  7.2 80.4 %copy-start.12 = (bf16[2,128,1536]{2,1,0:T(8,128)(2,1)S(1)}, bf16[2,128,1536]{2,1,0:T(8,128)(2,1)}, u32[]{:S(2)}) copy-start(bf16[2,128,1536]{2,1,0:T(8,128)(2,1)} %param.35) | copy-start | bytes 2359300
  7.2 80.4 %copy-start.127 = (f32[1536]{0:T(1024)S(1)}, f32[1536]{0:T(1024)}, u32[]{:S(2)}) copy-start(f32[1536]{0:T(1024)} %param.37) | copy-start | bytes 18436
  7.2 145.4 %all-gather.10.cloned.1.call-start = ((), (), s32[]{:S(2)}) async-start(), calls=%async_computation.16 | async-start | bytes 10543104 | tf_op jit(solution)/shard_map/all_gather | solution.py:162
  7.9 385.7 %all-gather.12.cloned.1.call-start = ((), (), s32[]{:S(2)}) async-start(), calls=%async_computation.17 | async-start | bytes 9732096 | tf_op jit(solution)/shard_map/all_gather | solution.py:161
  87.8 64.8 %copy-start.18 = (bf16[128,1536]{1,0:T(8,128)(2,1)}, bf16[128,1536]{1,0:T(8,128)(2,1)S(1)}, u32[]{:S(2)}) copy-start(bf16[128,1536]{1,0:T(8,128)(2,1)S(1)} %get-tuple-element.1191) | copy-start | bytes 1179652
  87.8 74.5 %copy-start.15 = (bf16[128,1536]{1,0:T(8,128)(2,1)}, bf16[128,1536]{1,0:T(8,128)(2,1)S(1)}, u32[]{:S(2)}) copy-start(bf16[128,1536]{1,0:T(8,128)(2,1)S(1)} %get-tuple-element.1190) | copy-start | bytes 1179652
  88.8 16.4 %all-to-all-start.4 = ((bf16[128,4,12]{0,2,1:T(8,128)(2,1)}), bf16[128,4,12]{0,2,1:T(8,128)(2,1)S(1)}, u32[]{:S(2)}, u32[]{:S(2)}) async-start(bf16[128,4,12]{0,2,1:T(8,128)(2,1)} %all_to_all.141), calls=%async_computation.4 | async-start | bytes 32768 | tf_op jit(solution)/shard_map/all_to_all | solution.py:196
  92.1 309.4 %all-gather.14.cloned.1.call-start = ((), (), s32[]{:S(2)}) async-start(), calls=%async_computation.18 | async-start | bytes 9732096 | tf_op jit(solution)/shard_map/all_gather | solution.py:164
  97.3 84.5 %copy-start.80 = (f32[3328]{0:T(1024)}, f32[3328]{0:T(1024)S(1)}, u32[]{:S(2)}) copy-start(f32[3328]{0:T(1024)S(1)} %get-tuple-element.1033) | copy-start | bytes 39940
  101.0 47.9 %copy-start.121 = (f32[2,256]{1,0:T(2,128)}, f32[2,256]{1,0:T(2,128)S(1)}, u32[]{:S(2)}) copy-start(f32[2,256]{1,0:T(2,128)S(1)} %get-tuple-element.1240) | copy-start | bytes 6148
  101.0 47.9 %copy-start.137 = (f32[2,256]{1,0:T(2,128)}, f32[2,256]{1,0:T(2,128)S(1)}, u32[]{:S(2)}) copy-start(f32[2,256]{1,0:T(2,128)S(1)} %get-tuple-element.1241) | copy-start | bytes 6148
  105.2 10.8 all-to-all-start.1
  159.3 7.4 collective-permute-start.1
  164.6 15.9 %collective-permute-start = (bf16[3,3328]{1,0:T(4,128)(2,1)}, bf16[3,3328]{1,0:T(4,128)(2,1)S(1)}, u32[]{:S(2)}, u32[]{:S(2)}) collective-permute-start(bf16[3,3328]{1,0:T(4,128)(2,1)} %slice.380), channel_id=1, source_target_pairs={{0,1},{1,2},{2,3},{3,4},{4,5},{5,6},{6,7},{7,8},{8,9},{9,10},{10,1... | collective-permute-start | bytes 59912 | tf_op jit(solution)/shard_map/ppermute | solution.py:19
  173.7 50.4 %all-to-all-start.3 = ((bf16[128,4,768]{0,2,1:T(8,128)(2,1)}), bf16[128,4,768]{0,2,1:T(8,128)(2,1)}, u32[]{:S(2)}, u32[]{:S(2)}) async-start(bf16[128,4,768]{0,2,1:T(8,128)(2,1)} %bitcast.581), calls=%async_computation.3 | async-start | bytes 1572864 | tf_op jit(solution)/shard_map/all_to_all | solution.py:195
  224.1 64.9 %all-to-all-start = ((bf16[128,4,768]{0,2,1:T(8,128)(2,1)}), bf16[128,4,768]{0,2,1:T(8,128)(2,1)}, u32[]{:S(2)}, u32[]{:S(2)}) async-start(bf16[128,4,768]{0,2,1:T(8,128)(2,1)} %bitcast.579), calls=%async_computation | async-start | bytes 1572864 | tf_op jit(solution)/shard_map/all_to_all | solution.py:195
  289.1 80.1 %all-to-all-start.5 = ((bf16[4,128,768]{1,2,0:T(8,128)(2,1)}), bf16[4,128,768]{1,2,0:T(8,128)(2,1)}, u32[]{:S(2)}, u32[]{:S(2)}) async-start(bf16[4,128,768]{1,2,0:T(8,128)(2,1)} %copy.441), calls=%async_computation.5 | async-start | bytes 1572864 | tf_op jit(solution)/shard_map/all_to_all | solution.py:221
  369.2 18.9 %all-to-all-start.2 = ((bf16[4,128,768]{1,2,0:T(8,128)(2,1)}), bf16[4,128,768]{1,2,0:T(8,128)(2,1)}, u32[]{:S(2)}, u32[]{:S(2)}) async-start(bf16[4,128,768]{1,2,0:T(8,128)(2,1)} %copy.425), calls=%async_computation.2 | async-start | bytes 1572864 | tf_op jit(solution)/shard_map/all_to_all | solution.py:221
  434.2 25.3 %all-to-all-start.9 = ((bf16[128,4,768]{0,2,1:T(8,128)(2,1)}), bf16[128,4,768]{0,2,1:T(8,128)(2,1)}, u32[]{:S(2)}, u32[]{:S(2)}) async-start(bf16[128,4,768]{0,2,1:T(8,128)(2,1)} %bitcast.580), calls=%async_computation.10 | async-start | bytes 1572864 | tf_op jit(solution)/shard_map/all_to_all | solution.py:282
  459.5 56.3 %all-to-all-start.6 = ((bf16[128,4,768]{0,2,1:T(8,128)(2,1)}), bf16[128,4,768]{0,2,1:T(8,128)(2,1)}, u32[]{:S(2)}, u32[]{:S(2)}) async-start(bf16[128,4,768]{0,2,1:T(8,128)(2,1)} %bitcast.84), calls=%async_computation.6 | async-start | bytes 1572864 | tf_op jit(solution)/shard_map/all_to_all | solution.py:282
  571.6 65.6 %copy-start.22 = (bf16[2,256,12,64]{1,0,3,2:T(2,128)(2,1)S(1)}, bf16[2,256,12,64]{1,0,3,2:T(2,128)(2,1)}, u32[]{:S(2)}) copy-start(bf16[2,256,12,64]{1,0,3,2:T(2,128)(2,1)} %all_to_all.156) | copy-start | bytes 2359300
  620.8 12.0 all-to-all-start.11
  632.9 15.1 %all-to-all-start.8 = ((bf16[4,128,12]{1,2,0:T(8,128)(2,1)}), bf16[4,128,12]{1,2,0:T(8,128)(2,1)}, u32[]{:S(2)}, u32[]{:S(2)}) async-start(bf16[4,128,12]{1,2,0:T(8,128)(2,1)} %copy.470), calls=%async_computation.9 | async-start | bytes 32768 | tf_op jit(solution)/shard_map/all_to_all | solution.py:319
  648.0 27.4 %all-to-all-start.10 = ((bf16[4,128,768]{1,2,0:T(8,128)(2,1)}), bf16[4,128,768]{1,2,0:T(8,128)(2,1)}, u32[]{:S(2)}, u32[]{:S(2)}) async-start(bf16[4,128,768]{1,2,0:T(8,128)(2,1)} %copy.484), calls=%async_computation.11 | async-start | bytes 1572864 | tf_op jit(solution)/shard_map/all_to_all | solution.py:316
  675.4 21.7 %all-to-all-start.7 = ((bf16[4,128,768]{1,2,0:T(8,128)(2,1)}), bf16[4,128,768]{1,2,0:T(8,128)(2,1)}, u32[]{:S(2)}, u32[]{:S(2)}) async-start(bf16[4,128,768]{1,2,0:T(8,128)(2,1)} %copy.456), calls=%async_computation.7 | async-start | bytes 1572864 | tf_op jit(solution)/shard_map/all_to_all | solution.py:316
  680.6 23.5 %reduce-scatter.7.cloned.1.call-start = ((), (), s32[]{:S(2)}) async-start(), calls=%async_computation.20 | async-start | bytes 327680 | tf_op jit(solution)/shard_map/reduce_scatter | solution.py:323
  683.6 41.1 %reduce-scatter.5.cloned.1.call-start = ((), (), s32[]{:S(2)}) async-start(), calls=%async_computation.19 | async-start | bytes 327680 | tf_op jit(solution)/shard_map/reduce_scatter | solution.py:323
  692.4 437.6 %reduce-scatter.9.cloned.1.call-start = ((), (), s32[]{:S(2)}) async-start(), calls=%async_computation.21 | async-start | bytes 41361408 | tf_op jit(solution)/shard_map/reduce_scatter | solution.py:371
  733.4 5.8 collective-permute-start.3
  735.3 6.4 collective-permute-start.2
  761.8 498.5 %all-reduce.31.cloned.1.call-start = ((), (), s32[]{:S(2)}) async-start(), calls=%async_computation.23 | async-start | bytes 183296 | tf_op jit(solution)/shard_map/psum | solution.py:388
  809.9 665.2 %reduce-scatter.11.cloned.1.call-start = ((), (), s32[]{:S(2)}) async-start(), calls=%async_computation.22 | async-start | bytes 19464192 | tf_op jit(solution)/shard_map/reduce_scatter | solution.py:380
  (182 other events, 1398.8 us)
Sparse Core Ops, SparseCore 0:
  10.8 90.7 all-gather.9
  104.4 90.3 all-gather.11
  197.6 94.1 all-gather.13
  683.9 20.1 reduce-scatter.6
  706.8 17.8 reduce-scatter.4
  761.9 368.0 reduce-scatter.8
  1137.6 122.5 all-reduce.30
  1267.2 207.8 reduce-scatter.10
where the time goes:
time: 1500 us; the launch traced here: 1490 us
  waiting for transfers between devices  684 us (46%)
  matrix products  216 us (14%)
  local copies, waits for them, and re-layouts  179 us (12%)
  blocking collectives  177 us (12%)
  other arithmetic  140 us (9%)
  starting transfers between devices  77 us (5%)
  between operations  17.4 us (1%)
    reduce_scatter x1, waiting for transfers between devices, shards(): lax.psum_scatter(lax.dot_general(part, proj_all, (((0,), (0,)), ((), ()))...  294 us
    reduce_scatter x1, waiting for transfers between devices, shards(): lax.psum_scatter(lax.dot_general(part, cot_all, (((0,), (0,)), ((), ())),...  215 us
    psum x1, waiting for transfers between devices, shards(): lax.psum((norm_total, taps_total, cbias_total, dtb_total, alog_total, ski...  125 us
    all_gather x1, blocking collectives, fetch(): lax.all_gather(dt_proj, ('dp', 'ctx', 'hd'), axis=0, tiled=True)  76.8 us
    all_gather x6, blocking collectives, carried_in(): lax.all_gather(part.astype(kind), axis)  67.1 us
    dot_general x8, matrix products, back_dot(): lax.dot_general(grad_val, weight, (((1,), (1,)), ((), ())), preferred_ele...  54.5 us
    dot_general x6, matrix products, block_ssd(): y_part = jnp.einsum('ctsh,cshp->cthp', mix_w, x_groups, precision=HIGH)  37.6 us
    all_gather x2, blocking collectives, shards(): bc_all = lax.all_gather(bc_low, 'hd', axis=0, tiled=True)  32.6 us
  transfers between devices with their start and end apart: 24, of which 10 were waited for; matrix products, arithmetic and copies ran while one was open for 24% of the time, Pallas kernels for 0%

commit v1 on v0

--- a/solution.py
+++ b/solution.py
@@ -195,7 +195,24 @@
             lax.all_to_all(x_low, "hd", split_axis=1, concat_axis=0, tiled=True),
             lax.all_to_all(rate_raw, "hd", split_axis=1, concat_axis=0, tiled=True),
         )
-        bc_all = lax.all_gather(bc_low, "hd", axis=0, tiled=True)
+        ways, here, step = (lax.axis_size("hd"), lax.axis_index("hd"), bc_low.shape[0])
+        shape = [n * ways if d == 0 else n for d, n in enumerate(bc_low.shape)]
+        bc_all = lax.dynamic_update_slice_in_dim(
+            jnp.zeros(shape, bc_low.dtype), bc_low, here * step, axis=0
+        )
+        going_up = going_down = bc_low
+        for far in range(1, ways // 2 + 1):
+            going_up = lax.ppermute(going_up, "hd", [(d, (d + 1) % ways) for d in range(ways)])
+            bc_all = lax.dynamic_update_slice_in_dim(
+                bc_all, going_up, (here - far) % ways * step, axis=0
+            )
+            if 2 * far < ways:
+                going_down = lax.ppermute(
+                    going_down, "hd", [(d, (d - 1) % ways) for d in range(ways)]
+                )
+                bc_all = lax.dynamic_update_slice_in_dim(
+                    bc_all, going_down, (here + far) % ways * step, axis=0
+                )
         x_float = x_heads.astype(jnp.float32)
         rate_float = rate_heads.astype(jnp.float32)
         bc_float = bc_all.astype(jnp.float32)

time: 1500 us -> 1450 us (0.967)
  blocking collectives: 177 us -> 145 us
  local copies, waits for them, and re-layouts: 179 us -> 159 us
    all_gather x2 -> x0, blocking collectives: 32.6 us -> none  [shards(): bc_all = lax.all_gather(bc_low, 'hd', axis=0, tiled=True)]
    another operation x26 -> x27, other arithmetic: 31.9 us -> 24.6 us
  transfers between devices with their start and end apart: 24 -> 30, of which waited for: 10 -> 13; matrix products, arithmetic and copies ran while one was open for 24% -> 26% of each run, Pallas kernels for 0% -> 0%
where the time goes in v1:
time: 1450 us; the launch traced here: 1430 us
  waiting for transfers between devices  686 us (47%)
  matrix products  220 us (15%)
  local copies, waits for them, and re-layouts  159 us (11%)
  blocking collectives  145 us (10%)
  other arithmetic  129 us (9%)
  starting transfers between devices  75.3 us (5%)
  between operations  17.3 us (1%)
    reduce_scatter x1, waiting for transfers between devices, shards(): lax.psum_scatter(lax.dot_general(part, proj_all, (((0,), (0,)), ((), ()))...  293 us
    reduce_scatter x1, waiting for transfers between devices, shards(): lax.psum_scatter(lax.dot_general(part, cot_all, (((0,), (0,)), ((), ())),...  215 us
    psum x1, waiting for transfers between devices, shards(): lax.psum((norm_total, taps_total, cbias_total, dtb_total, alog_total, ski...  125 us
    all_gather x1, blocking collectives, fetch(): lax.all_gather(dt_proj, ('dp', 'ctx', 'hd'), axis=0, tiled=True)  76.8 us
    all_gather x6, blocking collectives, carried_in(): lax.all_gather(part.astype(kind), axis)  68.4 us
    dot_general x8, matrix products, back_dot(): lax.dot_general(grad_val, weight, (((1,), (1,)), ((), ())), preferred_ele...  55.9 us
    dot_general x6, matrix products, block_ssd(): y_part = jnp.einsum('ctsh,cshp->cthp', mix_w, x_groups, precision=HIGH)  39.7 us
  transfers between devices with their start and end apart: 30, of which 13 were waited for; matrix products, arithmetic and copies ran while one was open for 26% of the time, Pallas kernels for 0%

profile of v1, /device:TPU:0, one launch (start us, length us, event | category | flops | bytes accessed | tf_op | source)
XLA Modules:
  0.0 1432.6 jit_solution(15815721886582029871)
XLA Ops:
  8.7 76.8 %all_gather.29 = bf16[1536,48]{1,0:T(8,128)(2,1)S(1)} all-gather(bf16[48,48]{1,0:T(8,128)(2,1)} %param.40), channel_id=1, replica_groups=mesh['dp'=2,'ctx'=4,'hd'=4] {'dp','ctx','hd'}, dimensions={0}, use_global_device_ids=true | all-gather | bytes 152064 | tf_op jit(solution)/shard_map/all_gather | solution.py:163
  126.1 14.2 all-gather.5
  151.0 6.8 convolution_convert_fusion
  223.4 7.8 while.156
  232.2 13.3 all-gather.1
  245.6 7.1 while.157
  252.8 6.6 fusion.24
  289.6 7.8 while.154
  298.4 12.0 all-gather
  310.4 7.5 fusion.31
  317.9 7.0 while.155
  372.2 7.3 multiply_reduce_fusion.19
  380.1 9.3 multiply_reduce_fusion.13
  389.4 7.1 multiply_reduce_fusion.18
  396.6 9.1 multiply_convert_fusion.3
  424.4 8.8 all-to-all-done.9
  445.9 10.8 all-gather.3
  470.2 7.8 while.153
  484.9 6.4 fusion.53
  499.8 11.6 all-gather.2
  577.2 6.5 fusion.116
  595.8 6.4 fusion.109
  650.5 16.4 %reduce-scatter.5.cloned.1.call-done = bf16[128,256]{1,0:T(8,128)(2,1)} async-done(((bf16[512,256]{1,0:T(8,128)(2,1)}), bf16[128,256]{1,0:T(8,128)(2,1)}) %reduce-scatter.5.cloned.1.call-update) | async-done | bytes 65552 | tf_op jit(solution)/shard_map/reduce_scatter | solution.py:340
  683.2 20.1 %fusion.38 = f32[1536,6448]{1,0:T(8,128)} fusion(bf16[128,48]{1,0:T(8,128)(2,1)S(1)} %copy.500, bf16[128,3328]{1,0:T(8,128)(2,1)S(1)} %fusion.98, bf16[128,3072]{1,0:T(8,128)(2,1)} %get-tuple-element.1177, bf16[128,48]{1,0:T(8,128)(2,1)S(1)} %copy.499, bf16[128,3328]{1,0:T(8,128)(2,1)S(1)} %fusion.99, bf16[128,3072]{1,0:T(8,128)(2,1)} %get-tuple-element.1175, ...), kind=kOutput, calls=%fused_computation.78 | convolution fusion | flops 5092294656 | bytes 43704320 | tf_op jit(solution)/shard_map/dot_general | solution.py:389
  706.0 7.9 fusion.276
  713.9 9.4 fusion.274
  730.4 9.3 convolution_add_fusion.2
  741.0 9.2 convolution_add_fusion.3
  752.4 11.7 fusion.118
  778.7 292.8 %reduce-scatter.9.cloned.1.call-done = f32[48,6448]{1,0:T(8,128)} async-done(((f32[1536,6448]{1,0:T(8,128)}), f32[48,6448]{1,0:T(8,128)}) %reduce-scatter.9.cloned.1.call-update) | async-done | bytes 1238032 | tf_op jit(solution)/shard_map/reduce_scatter | solution.py:388
  1076.7 125.0 %all-reduce.31.cloned.1.call-done = (f32[1536]{0:T(1024)}, f32[4,3328]{1,0:T(4,128)}, f32[3328]{0:T(1024)}, f32[48]{0:T(128)}, f32[48]{0:T(128)}, /*index=5*/f32[48]{0:T(128)}, f32[3072]{0:T(1024)}) async-done(((f32[1536]{0:T(1024)}, f32[4,3328]{1,0:T(4,128)}, f32[3328]{0:T(1024)}, f32[48]{0:T(128)}, f32[48]{0:T(128)}, /*index=5*/f32[48]{0:T(128)}, f32[3072]{0:T(1024)}), (f32[1536]{0:T(1024)}, ...) | async-done | bytes 85584 | tf_op jit(solution)/shard_map/psum | solution.py:405
  1201.7 214.8 %reduce-scatter.11.cloned.1.call-done = f32[96,1536]{1,0:T(8,128)} async-done(((f32[3072,1536]{1,0:T(8,128)}), f32[96,1536]{1,0:T(8,128)}) %reduce-scatter.11.cloned.1.call-update) | async-done | bytes 589840 | tf_op jit(solution)/shard_map/reduce_scatter | solution.py:397
  (821 shorter events, 499.7 us)
Async XLA Ops:
  7.2 79.9 %copy-start.12 = (bf16[2,128,1536]{2,1,0:T(8,128)(2,1)S(1)}, bf16[2,128,1536]{2,1,0:T(8,128)(2,1)}, u32[]{:S(2)}) copy-start(bf16[2,128,1536]{2,1,0:T(8,128)(2,1)} %param.35) | copy-start | bytes 2359300
  7.2 79.9 %copy-start.102 = (f32[1536]{0:T(1024)S(1)}, f32[1536]{0:T(1024)}, u32[]{:S(2)}) copy-start(f32[1536]{0:T(1024)} %param.37) | copy-start | bytes 18436
  7.2 143.8 %all-gather.10.cloned.1.call-start = ((), (), s32[]{:S(2)}) async-start(), calls=%async_computation.16 | async-start | bytes 10543104 | tf_op jit(solution)/shard_map/all_gather | solution.py:162
  7.9 364.2 %all-gather.12.cloned.1.call-start = ((), (), s32[]{:S(2)}) async-start(), calls=%async_computation.17 | async-start | bytes 9732096 | tf_op jit(solution)/shard_map/all_gather | solution.py:161
  88.5 16.2 %all-to-all-start.4 = ((bf16[128,4,12]{0,2,1:T(8,128)(2,1)}), bf16[128,4,12]{0,2,1:T(8,128)(2,1)S(1)}, u32[]{:S(2)}, u32[]{:S(2)}) async-start(bf16[128,4,12]{0,2,1:T(8,128)(2,1)} %all_to_all.141), calls=%async_computation.4 | async-start | bytes 32768 | tf_op jit(solution)/shard_map/all_to_all | solution.py:196
  91.8 288.2 %all-gather.14.cloned.1.call-start = ((), (), s32[]{:S(2)}) async-start(), calls=%async_computation.18 | async-start | bytes 9732096 | tf_op jit(solution)/shard_map/all_gather | solution.py:164
  104.7 10.8 all-to-all-start.1
  158.0 5.6 collective-permute-start.4
  161.6 6.3 collective-permute-start
  167.1 25.6 %collective-permute-start.5 = (bf16[128,256]{1,0:T(8,128)(2,1)}, bf16[128,256]{1,0:T(8,128)(2,1)}, u32[]{:S(2)}, u32[]{:S(2)}) collective-permute-start(bf16[128,256]{1,0:T(8,128)(2,1)} %get-tuple-element.1192), channel_id=1, source_target_pairs={{0,1},{1,2},{2,3},{3,0},{4,5},{5,6},{6,7},{7,4},{8,9},{9,10},{10,1... | collective-permute-start | bytes 196616 | tf_op jit(solution)/shard_map/ppermute | solution.py:205
  172.2 22.5 %collective-permute-start.1 = (bf16[128,256]{1,0:T(8,128)(2,1)}, bf16[128,256]{1,0:T(8,128)(2,1)}, u32[]{:S(2)}, u32[]{:S(2)}) collective-permute-start(bf16[128,256]{1,0:T(8,128)(2,1)} %get-tuple-element.1190), channel_id=1, source_target_pairs={{0,1},{1,2},{2,3},{3,0},{4,5},{5,6},{6,7},{7,4},{8,9},{9,10},{10,1... | collective-permute-start | bytes 196616 | tf_op jit(solution)/shard_map/ppermute | solution.py:205
  178.9 20.3 %collective-permute-start.6 = (bf16[128,256]{1,0:T(8,128)(2,1)}, bf16[128,256]{1,0:T(8,128)(2,1)S(1)}, u32[]{:S(2)}, u32[]{:S(2)}) collective-permute-start(bf16[128,256]{1,0:T(8,128)(2,1)} %get-tuple-element.1192), channel_id=1, source_target_pairs={{0,3},{1,0},{2,1},{3,2},{4,7},{5,4},{6,5},{7,6},{8,11},{9,8},{10,9... | collective-permute-start | bytes 196616 | tf_op jit(solution)/shard_map/ppermute | solution.py:210
  180.9 18.9 %collective-permute-start.2 = (bf16[128,256]{1,0:T(8,128)(2,1)}, bf16[128,256]{1,0:T(8,128)(2,1)S(1)}, u32[]{:S(2)}, u32[]{:S(2)}) collective-permute-start(bf16[128,256]{1,0:T(8,128)(2,1)} %get-tuple-element.1190), channel_id=1, source_target_pairs={{0,3},{1,0},{2,1},{3,2},{4,7},{5,4},{6,5},{7,6},{8,11},{9,8},{10,9... | collective-permute-start | bytes 196616 | tf_op jit(solution)/shard_map/ppermute | solution.py:210
  186.2 22.9 %all-to-all-start.3 = ((bf16[128,4,768]{0,2,1:T(8,128)(2,1)}), bf16[128,4,768]{0,2,1:T(8,128)(2,1)}, u32[]{:S(2)}, u32[]{:S(2)}) async-start(bf16[128,4,768]{0,2,1:T(8,128)(2,1)} %bitcast.580), calls=%async_computation.3 | async-start | bytes 1572864 | tf_op jit(solution)/shard_map/all_to_all | solution.py:195
  192.7 10.8 collective-permute-start.7
  194.7 9.5 collective-permute-start.3
  209.1 66.3 %all-to-all-start = ((bf16[128,4,768]{0,2,1:T(8,128)(2,1)}), bf16[128,4,768]{0,2,1:T(8,128)(2,1)}, u32[]{:S(2)}, u32[]{:S(2)}) async-start(bf16[128,4,768]{0,2,1:T(8,128)(2,1)} %bitcast.579), calls=%async_computation | async-start | bytes 1572864 | tf_op jit(solution)/shard_map/all_to_all | solution.py:195
  275.4 71.3 %all-to-all-start.5 = ((bf16[4,128,768]{1,2,0:T(8,128)(2,1)}), bf16[4,128,768]{1,2,0:T(8,128)(2,1)}, u32[]{:S(2)}, u32[]{:S(2)}) async-start(bf16[4,128,768]{1,2,0:T(8,128)(2,1)} %copy.441), calls=%async_computation.5 | async-start | bytes 1572864 | tf_op jit(solution)/shard_map/all_to_all | solution.py:238
  346.7 20.0 %all-to-all-start.2 = ((bf16[4,128,768]{1,2,0:T(8,128)(2,1)}), bf16[4,128,768]{1,2,0:T(8,128)(2,1)}, u32[]{:S(2)}, u32[]{:S(2)}) async-start(bf16[4,128,768]{1,2,0:T(8,128)(2,1)} %copy.425), calls=%async_computation.2 | async-start | bytes 1572864 | tf_op jit(solution)/shard_map/all_to_all | solution.py:238
  413.0 20.1 %all-to-all-start.9 = ((bf16[128,4,768]{0,2,1:T(8,128)(2,1)}), bf16[128,4,768]{0,2,1:T(8,128)(2,1)}, u32[]{:S(2)}, u32[]{:S(2)}) async-start(bf16[128,4,768]{0,2,1:T(8,128)(2,1)} %bitcast.581), calls=%async_computation.10 | async-start | bytes 1572864 | tf_op jit(solution)/shard_map/all_to_all | solution.py:299
  433.2 58.1 %all-to-all-start.6 = ((bf16[128,4,768]{0,2,1:T(8,128)(2,1)}), bf16[128,4,768]{0,2,1:T(8,128)(2,1)}, u32[]{:S(2)}, u32[]{:S(2)}) async-start(bf16[128,4,768]{0,2,1:T(8,128)(2,1)} %bitcast.84), calls=%async_computation.6 | async-start | bytes 1572864 | tf_op jit(solution)/shard_map/all_to_all | solution.py:299
  562.8 10.7 all-to-all-start.11
  573.5 17.3 %all-to-all-start.8 = ((bf16[4,128,12]{1,2,0:T(8,128)(2,1)}), bf16[4,128,12]{1,2,0:T(8,128)(2,1)S(1)}, u32[]{:S(2)}, u32[]{:S(2)}) async-start(bf16[4,128,12]{1,2,0:T(8,128)(2,1)} %copy.470), calls=%async_computation.9 | async-start | bytes 32768 | tf_op jit(solution)/shard_map/all_to_all | solution.py:336
  590.8 26.8 %all-to-all-start.10 = ((bf16[4,128,768]{1,2,0:T(8,128)(2,1)}), bf16[4,128,768]{1,2,0:T(8,128)(2,1)}, u32[]{:S(2)}, u32[]{:S(2)}) async-start(bf16[4,128,768]{1,2,0:T(8,128)(2,1)} %copy.484), calls=%async_computation.11 | async-start | bytes 1572864 | tf_op jit(solution)/shard_map/all_to_all | solution.py:333
  617.5 21.3 %all-to-all-start.7 = ((bf16[4,128,768]{1,2,0:T(8,128)(2,1)}), bf16[4,128,768]{1,2,0:T(8,128)(2,1)}, u32[]{:S(2)}, u32[]{:S(2)}) async-start(bf16[4,128,768]{1,2,0:T(8,128)(2,1)} %copy.456), calls=%async_computation.7 | async-start | bytes 1572864 | tf_op jit(solution)/shard_map/all_to_all | solution.py:333
  622.8 23.5 %reduce-scatter.7.cloned.1.call-start = ((), (), s32[]{:S(2)}) async-start(), calls=%async_computation.20 | async-start | bytes 327680 | tf_op jit(solution)/shard_map/reduce_scatter | solution.py:340
  625.0 41.9 %reduce-scatter.5.cloned.1.call-start = ((), (), s32[]{:S(2)}) async-start(), calls=%async_computation.19 | async-start | bytes 327680 | tf_op jit(solution)/shard_map/reduce_scatter | solution.py:340
  636.2 435.3 %reduce-scatter.9.cloned.1.call-start = ((), (), s32[]{:S(2)}) async-start(), calls=%async_computation.21 | async-start | bytes 41361408 | tf_op jit(solution)/shard_map/reduce_scatter | solution.py:388
  674.8 5.8 collective-permute-start.9
  676.7 6.4 collective-permute-start.8
  703.4 498.3 %all-reduce.31.cloned.1.call-start = ((), (), s32[]{:S(2)}) async-start(), calls=%async_computation.23 | async-start | bytes 183296 | tf_op jit(solution)/shard_map/psum | solution.py:405
  752.4 664.2 %reduce-scatter.11.cloned.1.call-start = ((), (), s32[]{:S(2)}) async-start(), calls=%async_computation.22 | async-start | bytes 19464192 | tf_op jit(solution)/shard_map/reduce_scatter | solution.py:397
  (167 other events, 1563.2 us)
Sparse Core Ops, SparseCore 0:
  10.8 90.7 all-gather.9
  104.4 89.4 all-gather.11
  196.7 92.5 all-gather.13
  626.1 20.0 reduce-scatter.6
  649.0 17.8 reduce-scatter.4
  703.5 367.9 reduce-scatter.8
  1079.1 122.5 all-reduce.30
  1208.7 207.8 reduce-scatter.10
